TPU v7x, 32 devices: a whole 2x2x4 slice. The times are simulated.
32 devices in a mesh: region: 4 (over y, x), col: 8 (over z, core).
Axes of the slice: x: 2, y: 2, z: 4, core: 2. Of those that a mesh axis runs over, the one named last changes fastest.
Arguments:
- jac: bfloat16 [256, 128], P(('region', 'col')), may hold values from -2 to 2
- dest: int32 [256, 2], P(('region', 'col')), may hold values from 0 to 3, all different within a row; in each aligned block of 8 rows (0 to 7, 8 to 15, ...) at most 6 rows name the same one
- near_pose: int32 [256, 2], P(('region', 'col')), may hold values from 0 to 255
- prior: float32 [8192], P('region'), may hold values from 0.5 to 8
Outputs:
- front_out: float32 [8192, 8192], P('region', 'col')
Inputs may be any that keep to these rules, and one draw needn't show every extreme that they name: `dest`: each row names two different regions; among the 8 rows of one device no region is named more than 6 times, and in some device's rows some region is named exactly 6 times.
All inputs are finite; a program needn't handle non-finite values.
Results may differ from a plain program's by a relative error of at most 0.00045.
Values may be sent and summed in bfloat16 or wider, within the bound.
No kernel may reach another device: no remote copies, remote signals or barrier semaphores. Data moves between devices by JAX's collectives and lax.ppermute only.
A program may use at most 320 MiB of HBM per device.

v0:
```python
import jax
import jax.numpy as jnp
from jax import lax
from jax.sharding import PartitionSpec as P

NB = 128
K_PANELS = 2


def broadcast(block, axis, owner):
    block = jnp.where(lax.axis_index(axis) == owner, block, jnp.zeros_like(block))
    return lax.psum(block, axis)


def placed(pose_pair, blocks, first_pose, pose_count):
    pose_grid = first_pose + jnp.arange(pose_count, dtype=jnp.int32)
    summed = jnp.zeros((blocks.shape[0], 8, pose_count, 8), jnp.float32)
    for endpoint in range(2):
        matches = (pose_pair[:, endpoint][:, None] == pose_grid[None, :]).astype(jnp.float32)
        summed = summed + matches[:, None, :, None] * blocks[:, endpoint][:, :, None, :]
    return summed.astype(jnp.bfloat16).reshape(blocks.shape[0] * 8, pose_count * 8)


def body(jac, dest, near_pose, prior):
    regions = lax.axis_size("region")
    columns = lax.axis_size("col")
    region_index = lax.axis_index("region")
    column_index = lax.axis_index("col")
    count_rows = jac.shape[0]
    row_block = prior.shape[0]
    front = row_block * regions
    col_block = front // columns
    region_poses = front // 8 // regions
    capacity = max(2, 3 * count_rows // regions)
    slots_out = regions * capacity
    targets = dest.reshape(-1)
    member = (targets[:, None] == jnp.arange(regions, dtype=jnp.int32)[None, :]).astype(jnp.int32)
    ranking = jnp.sum(jnp.cumsum(member, axis=0) * member, axis=1) - 1
    position = targets * capacity + ranking
    placing = (position[None, :] == jnp.arange(slots_out, dtype=jnp.int32)[:, None]).astype(
        jnp.bfloat16
    )
    copies = jnp.repeat(jac, 2, axis=0)
    labels = jnp.concatenate([near_pose // 64, near_pose % 64, dest], axis=1).astype(jnp.bfloat16)
    label_copies = jnp.repeat(labels, 2, axis=0)
    packed = (
        jnp.dot(placing, copies, preferred_element_type=jnp.float32)
        .astype(jnp.bfloat16)
        .reshape(regions, capacity, 128)
    )
    packed_labels = (
        jnp.dot(placing, label_copies, preferred_element_type=jnp.float32)
        .astype(jnp.bfloat16)
        .reshape(regions, capacity, 6)
    )
    arrived, arrived_labels = (
        lax.all_to_all(packed, "region", split_axis=0, concat_axis=0, tiled=True),
        lax.all_to_all(packed_labels, "region", split_axis=0, concat_axis=0, tiled=True),
    )
    piece_rows = lax.all_gather(arrived, "col", axis=0, tiled=True)
    piece_labels = lax.all_gather(arrived_labels, "col", axis=0, tiled=True)
    slot_count = piece_rows.shape[0] * piece_rows.shape[1]
    blocks = piece_rows.reshape(slot_count, 2, 8, 8).astype(jnp.float32)
    label_values = piece_labels.reshape(slot_count, 6).astype(jnp.int32)
    near_values = label_values[:, 0:2] * 64 + label_values[:, 2:4]
    pose_pair = label_values[:, 4:6] * region_poses + near_values
    own_rows = placed(pose_pair, blocks, region_index * region_poses, region_poses)
    own_cols = placed(pose_pair, blocks, column_index * (col_block // 8), col_block // 8)
    matrix = lax.dot_general(
        own_rows, own_cols, (((0,), (0,)), ((), ())), preferred_element_type=jnp.float32
    )
    row_global = region_index * row_block + jnp.arange(row_block, dtype=jnp.int32)
    col_global = column_index * col_block + jnp.arange(col_block, dtype=jnp.int32)
    matrix = matrix + jnp.where(row_global[:, None] == col_global[None, :], prior[:, None], 0.0)
    for panel_number in range(K_PANELS):
        low_edge = panel_number * NB
        high_edge = low_edge + NB
        owner_col = low_edge // col_block
        offset_col = low_edge - owner_col * col_block
        local_panel = lax.slice_in_dim(matrix, offset_col, offset_col + NB, axis=1)
        panel_part = broadcast(local_panel.astype(jnp.bfloat16), "col", owner_col).astype(
            local_panel.dtype
        )
        whole_panel = lax.all_gather(
            panel_part.astype(jnp.bfloat16), "region", axis=0, tiled=True
        ).astype(panel_part.dtype)
        diagonal = lax.slice_in_dim(whole_panel, low_edge, high_edge, axis=0)
        their_rows = lax.dynamic_slice_in_dim(
            whole_panel, column_index * col_block, col_block, axis=0
        )
        factor = jnp.tril(jnp.linalg.cholesky(diagonal))
        panel_cols = low_edge + jnp.arange(NB, dtype=jnp.int32)

        def finish(block_rows, global_rows):
            solved = jax.scipy.linalg.solve_triangular(factor, block_rows.T, lower=True).T
            keeping = global_rows[:, None] >= panel_cols[None, :]
            return jnp.where(keeping, solved, 0.0)

        mine = finish(panel_part, row_global)
        theirs = finish(their_rows, col_global)
        matrix = matrix - jnp.dot(mine, theirs.T, precision=lax.Precision.HIGHEST)
        with_panel = matrix.at[:, offset_col : offset_col + NB].set(mine)
        matrix = jnp.where(column_index == owner_col, with_panel, matrix)
        in_panel = (row_global >= low_edge) & (row_global < high_edge)
        right_side = col_global >= high_edge
        matrix = jnp.where(in_panel[:, None] & right_side[None, :], 0.0, matrix)
    return matrix


def solution(mesh):
    return jax.shard_map(
        body,
        mesh=mesh,
        in_specs=(
            P(("region", "col"), None),
            P(("region", "col"), None),
            P(("region", "col"), None),
            P("region"),
        ),
        out_specs=P("region", "col"),
        check_vma=False,
    )
```

profile of v0, /device:TPU:0, one launch (start us, length us, event | category | flops | bytes accessed | tf_op | source)
XLA Modules:
  0.0 650.6 jit_solution(2428502559729770655)
XLA Ops:
  6.5 0.8 copy.32
  7.3 0.7 convert.21
  8.2 0.2 select_reduce_fusion.2
  8.4 0.7 fusion.41
  9.1 0.1 copy.33
  9.2 0.2 convolution_convert_fusion.1
  9.5 0.6 copy.34
  10.1 5.2 all-to-all-start
  15.3 0.1 convolution_convert_fusion
  15.4 0.6 reshape.292
  16.0 3.9 all-to-all-done
  19.9 3.2 all-to-all-start.1
  23.3 0.1 copy.35
  23.4 14.2 %all_gather.12 = bf16[32,6,6]{2,1,0:T(8,128)(2,1)S(1)} all-gather(bf16[4,6,6]{2,1,0:T(8,128)(2,1)S(1)} %copy.35), channel_id=1, replica_groups=mesh['region'=4,'col'=8] {'col'}, dimensions={0}, use_global_device_ids=true | all-gather | bytes 2592 | tf_op jit(solution)/shard_map/all_gather | solution.py:61
  37.6 0.1 copy.36
  37.7 0.1 copy.37
  37.8 0.1 reshape.293
  38.0 0.1 compare_convert_fusion.1
  38.1 0.8 compare_convert_fusion.3
  38.9 14.0 %all_gather.13 = bf16[32,6,128]{2,1,0:T(8,128)(2,1)S(1)} all-gather(bf16[4,6,128]{2,1,0:T(8,128)(2,1)S(1)} %all-to-all-done.1), channel_id=1, replica_groups=mesh['region'=4,'col'=8] {'col'}, dimensions={0}, use_global_device_ids=true | all-gather | bytes 55296 | tf_op jit(solution)/shard_map/all_gather | solution.py:60
  52.9 0.8 reshape.294
  53.7 0.1 slice_bitcast_fusion.1
  53.9 43.1 %add_convert_fusion = bf16[192,8,256,8]{3,2,1,0:T(8,128)(2,1)} fusion(f32[192,8,8]{2,1,0:T(8,128)S(1)} %get-tuple-element.33, f32[192,256]{1,0:T(8,128)S(1)} %get-tuple-element.37, f32[192,8,8]{2,1,0:T(8,128)S(1)} %get-tuple-element.32, f32[192,256]{1,0:T(8,128)S(1)} %get-tuple-element.36), kind=kLoop, calls=%fused_computation | loop fusion | flops 12582912 | bytes 6782976 | tf_op jit(solution)/shard_map/convert_element_type | solution.py:21
  96.9 141.8 %convert_element_type.99 = bf16[1536,2048]{1,0:T(8,128)(2,1)} reshape(bf16[192,8,256,8]{3,2,1,0:T(8,128)(2,1)} %add_convert_fusion) | data formatting | bytes 12582912 | tf_op jit(solution)/shard_map/convert_element_type | solution.py:21
  238.7 23.6 %add_convert_fusion.1 = bf16[192,8,128,8]{3,2,1,0:T(8,128)(2,1)} fusion(f32[192,8,8]{2,1,0:T(8,128)S(1)} %get-tuple-element.33, f32[192,128]{1,0:T(8,128)S(1)} %copy-done.9, f32[192,8,8]{2,1,0:T(8,128)S(1)} %get-tuple-element.32, f32[192,128]{1,0:T(8,128)S(1)} %copy-done.8), kind=kLoop, calls=%fused_computation.1 | loop fusion | flops 6291456 | bytes 3440640 | tf_op jit(solution)/shard_map/convert_element_type | solution.py:21
  262.3 71.0 %convert_element_type.103 = bf16[1536,1024]{1,0:T(8,128)(2,1)S(1)} reshape(bf16[192,8,128,8]{3,2,1,0:T(8,128)(2,1)} %add_convert_fusion.1) | data formatting | bytes 6291456 | tf_op jit(solution)/shard_map/convert_element_type | solution.py:21
  333.3 9.5 %select_add_fusion = f32[2048,1024]{0,1:T(8,128)S(1)} fusion(f32[2048]{0:T(1024)S(1)} %copy-done.10, s32[2048]{0:T(1024)S(1)} %iota_add_fusion, s32[1024]{0:T(1024)S(1)} %iota_add_fusion.1, bf16[1536,2048]{1,0:T(8,128)(2,1)} %convert_element_type.99, bf16[1536,1024]{1,0:T(8,128)(2,1)S(1)} %convert_element_type.103), kind=kOutput, calls=%fused_computation.2 | convolution fusion | flops 6448742400 | bytes 17846272 | tf_op jit(solution)/shard_map/dot_general | solution.py:69
  342.8 3.4 copy-done.3
  346.2 0.8 fusion.10
  347.1 58.0 %all-reduce.3.cloned.1.call-done = bf16[2048,128]{0,1:T(8,128)(2,1)} async-done(((bf16[2048,128]{0,1:T(8,128)(2,1)}), bf16[2048,128]{0,1:T(8,128)(2,1)}) %all-reduce.3.cloned.1.call-update) | async-done | bytes 524304 | tf_op jit(solution)/shard_map/psum | solution.py:12
  405.1 0.3 all-reduce.5.cloned.1.call-start
  405.4 0.6 compare_reduce_fusion.3
  406.1 35.1 %all-gather.3.cloned.1.call-done = bf16[8192,128]{0,1:T(8,128)(2,1)} async-done(((bf16[2048,128]{0,1:T(8,128)(2,1)}), bf16[8192,128]{0,1:T(8,128)(2,1)}) %all-gather.3.cloned.1.call-update) | async-done | bytes 2097168 | tf_op jit(solution)/shard_map/all_gather | solution.py:84
  441.2 0.8 slice.110
  442.1 2.0 convert_element_type.104
  444.1 1.9 copy-done.5
  446.0 11.7 %cholesky.44 = f32[128,128]{1,0:T(8,128)S(1)} custom-call(f32[128,128]{1,0:T(8,128)S(1)} %fusion.25), custom_call_target="Cholesky" | custom-call | tf_op jit(solution)/shard_map/jit(cholesky)/cholesky | solution.py:91
  457.8 0.7 compare_reduce_fusion.1
  458.5 0.6 fusion.18
  459.1 9.8 %custom-call.10 = f32[1,128,128]{1,2,0:T(8,128)S(1)} custom-call(f32[1,128,128]{2,1,0:T(8,128)S(1)} %fusion.18), custom_call_target="InvertDiagBlocksLowerTriangular" | custom-call | tf_op jit(solution)/shard_map/jit(_solve_triangular)/triangular_solve | solution.py:95
  469.0 1.7 fusion.3
  470.7 1.1 fusion.1
  471.7 19.5 %convolution_subtract_fusion.1 = f32[2048,1024]{0,1:T(8,128)S(1)} fusion(f32[2048,1024]{0,1:T(8,128)} %copy-done.3, f32[2048,128]{0,1:T(8,128)S(1)} %fusion.1, f32[1024,128]{0,1:T(8,128)S(1)} %fusion.3), kind=kOutput, calls=%fused_computation.6 | convolution fusion | flops 3223322624 | bytes 18350080 | tf_op jit(solution)/shard_map/dot_general | solution.py:101
  491.3 0.9 fusion.4
  492.2 0.9 and_select_fusion
  493.1 3.4 copy-done.2
  496.5 0.8 fusion.11
  497.4 56.6 %all-reduce.5.cloned.1.call-done = bf16[2048,128]{0,1:T(8,128)(2,1)} async-done(((bf16[2048,128]{0,1:T(8,128)(2,1)}), bf16[2048,128]{0,1:T(8,128)(2,1)}) %all-reduce.5.cloned.1.call-update) | async-done | bytes 524304 | tf_op jit(solution)/shard_map/psum | solution.py:12
  554.0 0.6 compare_reduce_fusion.2
  554.7 35.3 %all-gather.5.cloned.1.call-done = bf16[8192,128]{0,1:T(8,128)(2,1)} async-done(((bf16[2048,128]{0,1:T(8,128)(2,1)}), bf16[8192,128]{0,1:T(8,128)(2,1)}) %all-gather.5.cloned.1.call-update) | async-done | bytes 2097168 | tf_op jit(solution)/shard_map/all_gather | solution.py:84
  589.9 0.8 slice.113
  590.7 0.1 copy.41
  590.8 2.0 convert_element_type.105
  592.8 1.9 copy-done.4
  594.8 11.7 %cholesky.55 = f32[128,128]{1,0:T(8,128)S(1)} custom-call(f32[128,128]{1,0:T(8,128)S(1)} %fusion.22), custom_call_target="Cholesky" | custom-call | tf_op jit(solution)/shard_map/jit(cholesky)/cholesky | solution.py:91
  606.5 0.7 compare_reduce_fusion
  607.2 0.6 fusion.19
  607.9 9.8 %custom-call.12 = f32[1,128,128]{1,2,0:T(8,128)S(1)} custom-call(f32[1,128,128]{2,1,0:T(8,128)S(1)} %fusion.19), custom_call_target="InvertDiagBlocksLowerTriangular" | custom-call | tf_op jit(solution)/shard_map/jit(_solve_triangular)/triangular_solve | solution.py:95
  617.7 1.7 fusion.2
  619.4 1.1 fusion
  620.4 9.2 %convolution_subtract_fusion = f32[2048,1024]{0,1:T(8,128)S(1)} fusion(f32[2048,1024]{0,1:T(8,128)} %copy-done.2, f32[2048,128]{0,1:T(8,128)S(1)} %fusion, f32[1024,128]{0,1:T(8,128)S(1)} %fusion.2), kind=kOutput, calls=%fused_computation.5 | convolution fusion | flops 3223322624 | bytes 18350080 | tf_op jit(solution)/shard_map/dot_general | solution.py:101
  629.6 0.9 fusion.5
  630.5 4.1 and_select_fusion.1
  634.6 9.2 %copy.43 = f32[2048,1024]{1,0:T(8,128)} copy(f32[2048,1024]{0,1:T(8,128)} %and_select_fusion.1) | data formatting | bytes 16777216 | tf_op jit(solution)/shard_map/jit(_where)/select_n | solution.py:106
  (51 shorter events, 0.8 us)
Async XLA Ops:
  6.5 8.7 %copy-start = (bf16[8,128]{1,0:T(8,128)(2,1)S(1)}, bf16[8,128]{1,0:T(8,128)(2,1)}, u32[]{:S(2)}) copy-start(bf16[8,128]{1,0:T(8,128)(2,1)} %param.13) | copy-start | bytes 6148
  10.1 9.9 %all-to-all-start = ((bf16[4,6,6]{1,2,0:T(8,128)(2,1)}), bf16[4,6,6]{1,2,0:T(8,128)(2,1)S(1)}, u32[]{:S(2)}, u32[]{:S(2)}) async-start(bf16[4,6,6]{1,2,0:T(8,128)(2,1)} %copy.34), calls=%async_computation | async-start | bytes 16384 | tf_op jit(solution)/shard_map/all_to_all | solution.py:58
  19.9 19.0 %all-to-all-start.1 = ((bf16[4,6,128]{2,1,0:T(8,128)(2,1)}), bf16[4,6,128]{2,1,0:T(8,128)(2,1)S(1)}, u32[]{:S(2)}, u32[]{:S(2)}) async-start(bf16[4,6,128]{2,1,0:T(8,128)(2,1)} %reshape.292), calls=%async_computation.1 | async-start | bytes 16384 | tf_op jit(solution)/shard_map/all_to_all | solution.py:57
  23.2 381.9 %all-reduce.3.cloned.1.call-start = ((), (), s32[]{:S(2)}) async-start(), calls=%async_computation.2 | async-start | bytes 1048576 | tf_op jit(solution)/shard_map/psum | solution.py:12
  96.9 141.8 %copy-start.8 = (f32[192,128]{1,0:T(8,128)S(1)}, f32[192,128]{1,0:T(8,128)}, u32[]{:S(2)}) copy-start(f32[192,128]{1,0:T(8,128)} %get-tuple-element.40) | copy-start | bytes 294916
  96.9 141.8 %copy-start.9 = (f32[192,128]{1,0:T(8,128)S(1)}, f32[192,128]{1,0:T(8,128)}, u32[]{:S(2)}) copy-start(f32[192,128]{1,0:T(8,128)} %get-tuple-element.41) | copy-start | bytes 294916
  262.3 71.0 %copy-start.10 = (f32[2048]{0:T(1024)S(1)}, f32[2048]{0:T(1024)}, u32[]{:S(2)}) copy-start(f32[2048]{0:T(1024)} %param.16) | copy-start | bytes 24580
  342.8 3.4 copy-start.3
  347.1 94.2 %all-gather.3.cloned.1.call-start = ((), (), s32[]{:S(2)}) async-start(), calls=%async_computation.3 | async-start | bytes 2621440 | tf_op jit(solution)/shard_map/all_gather | solution.py:84
  405.1 65.5 %copy-start.6 = (bf16[2048,128]{0,1:T(8,128)(2,1)S(1)}, bf16[2048,128]{0,1:T(8,128)(2,1)}, u32[]{:S(2)}) copy-start(bf16[2048,128]{0,1:T(8,128)(2,1)} %all-reduce.3.cloned.1.call-done) | copy-start | bytes 1572868
  405.1 148.8 %all-reduce.5.cloned.1.call-start = ((), (), s32[]{:S(2)}) async-start(), calls=%async_computation.4 | async-start | bytes 1048576 | tf_op jit(solution)/shard_map/psum | solution.py:12
  444.1 1.9 copy-start.5
  493.1 3.4 copy-start.2
  497.3 92.6 %all-gather.5.cloned.1.call-start = ((), (), s32[]{:S(2)}) async-start(), calls=%async_computation.5 | async-start | bytes 2621440 | tf_op jit(solution)/shard_map/all_gather | solution.py:84
  554.0 65.4 %copy-start.7 = (bf16[2048,128]{0,1:T(8,128)(2,1)S(1)}, bf16[2048,128]{0,1:T(8,128)(2,1)}, u32[]{:S(2)}) copy-start(bf16[2048,128]{0,1:T(8,128)(2,1)} %all-reduce.5.cloned.1.call-done) | copy-start | bytes 1572868
  592.8 1.9 copy-start.4
  630.5 13.4 %copy-start.1 = (bf16[8,128]{1,0:T(8,128)(2,1)S(1)}, bf16[8,128]{1,0:T(8,128)(2,1)}, u32[]{:S(2)}) copy-start(bf16[8,128]{1,0:T(8,128)(2,1)} %param.13) | copy-start | bytes 6148
Sparse Core Ops, SparseCore 0:
  347.2 57.8 all-reduce.2
  407.0 34.2 all-gather.2
  497.5 56.4 all-reduce.4
  555.7 34.2 all-gather.4
where the time goes:
time: 654 us; the launch traced here: 651 us
  local copies, waits for them, and re-layouts  238 us (36%)
  waiting for transfers between devices  189 us (29%)
  other arithmetic  129 us (20%)
  matrix products  44 us (7%)
  blocking collectives  28.2 us (4%)
  between operations  13.6 us (2%)
  starting transfers between devices  8.86 us (1%)
    convert_element_type x2, local copies, waits for them, and re-layouts, placed(): summed.astype(jnp.bfloat16).reshape(blocks.shape[0] * 8, pose_count * 8)  213 us
    psum x2, waiting for transfers between devices, broadcast(): return lax.psum(block, axis)  115 us
    all_gather x2, waiting for transfers between devices, body(): lax.all_gather(panel_part.astype(jnp.bfloat16), 'region', axis=0, tiled=T...  70.4 us
    convert_element_type x2, other arithmetic, placed(): summed.astype(jnp.bfloat16).reshape(blocks.shape[0] * 8, pose_count * 8)  66.7 us
    dot_general x2, matrix products, body(): matrix = matrix - jnp.dot(mine, theirs.T, precision=lax.Precision.HIGHEST)  28.7 us
    another operation x6, other arithmetic, body(): factor = jnp.tril(jnp.linalg.cholesky(diagonal))  24.9 us
    another operation x4, other arithmetic, finish(): jax.scipy.linalg.solve_triangular(factor, block_rows.T, lower=True)  20.9 us
    all_gather x1, blocking collectives, body(): piece_labels = lax.all_gather(arrived_labels, 'col', axis=0, tiled=True)  14.2 us
  transfers between devices with their start and end apart: 6, of which 5 were waited for; matrix products, arithmetic and copies ran while one was open for 1% of the time, Pallas kernels for 0%

commit v1 on v0

v1 whole, which is shorter than its diff:
```python
import functools

import jax
import jax.numpy as jnp
from jax import lax
from jax.experimental import pallas as pl
from jax.experimental.pallas import tpu as pltpu
from jax.sharding import PartitionSpec as P

NB = 128
K_PANELS = 2
PANEL = NB * K_PANELS
PP = PANEL // 8
CH = 256
BIG = float(1 << 24)
f32, bf16, i32 = jnp.float32, jnp.bfloat16, jnp.int32


def iota(shape, dim):
    return lax.broadcasted_iota(i32, shape, dim)


def split(x, parts):
    out = []
    for _ in range(parts):
        top = x.astype(bf16)
        out.append(top)
        x = x - top.astype(f32)
    return out


def dot(a, b, dims=((1,), (0,))):
    return lax.dot_general(a, b, (dims, ((), ())), preferred_element_type=f32)


def pack_kernel(jac_ref, dest_ref, near_ref, prior_ref, out_ref):
    shape = (8, 128)
    lane, row = iota(shape, 1), iota(shape, 0)
    dest, near = dest_ref[...].astype(f32), near_ref[...].astype(f32)
    tile = jnp.zeros(shape, f32)
    for at, column in enumerate((dest[:, 0:1], near[:, 0:1], dest[:, 1:2], near[:, 1:2])):
        tile = jnp.where(lane == at, column, tile)
    first = prior_ref[0:2, :]
    both = jnp.where(row < 4, first[0:1, :], first[1:2, :])
    spread = jnp.zeros(shape, f32)
    for at in range(4):
        moved = both if at == 0 else pltpu.roll(both, 128 - 32 * at, 1)
        spread = jnp.where(row % 4 == at, moved, spread)
    for at, part in enumerate(split(spread, 3)):
        moved = pltpu.roll(part.astype(f32), 32 * (at + 1), 1)
        tile = jnp.where(lane // 32 == at + 1, moved, tile)
    whole = jnp.concatenate([jac_ref[...].astype(f32), tile], axis=0).astype(bf16)
    out_ref[...] = jnp.broadcast_to(whole[None], out_ref.shape)


def pack(jac, dest, near_pose, prior2, devices):
    return pl.pallas_call(
        pack_kernel,
        out_shape=jax.ShapeDtypeStruct((devices, 16, 128), bf16),
        name="pack",
    )(jac, dest, near_pose, prior2)


def fill_kernel(place, sizes, prior_ref, out_ref, zeros, squares, sem, sem2):
    rows, cols = sizes
    region, column = place()
    pieces = rows // zeros.shape[0]
    zeros[...] = jnp.zeros_like(zeros)
    step = zeros.shape[0]
    copies = [
        pltpu.make_async_copy(zeros, out_ref.at[pl.ds(at * step, step), :], sem.at[at])
        for at in range(pieces)
    ]
    for copy in copies:
        copy.start()
    start = column * cols - region * rows
    own = (start >= 0) & (start < rows)

    @pl.when(own)
    def _():
        diagonal = iota((128, 128), 0) == iota((128, 128), 1)
        first = start // 128
        for at in range(cols // 128):
            squares[at] = jnp.where(diagonal, prior_ref[pl.ds(first + at, 1), :], 0.0)

    for copy in copies:
        copy.wait()

    @pl.when(own)
    def _():
        base = pl.multiple_of(start, 128)
        patches = [
            pltpu.make_async_copy(
                squares.at[at],
                out_ref.at[pl.ds(base + at * 128, 128), pl.ds(at * 128, 128)],
                sem2.at[at],
            )
            for at in range(cols // 128)
        ]
        for patch in patches:
            patch.start()
        for patch in patches:
            patch.wait()


def fill(place, rows, cols, prior2):
    step = min(256, rows)
    return pl.pallas_call(
        functools.partial(fill_kernel, place, (rows, cols)),
        out_shape=jax.ShapeDtypeStruct((rows, cols), f32),
        out_specs=pl.BlockSpec(memory_space=pl.ANY),
        scratch_shapes=[
            pltpu.VMEM((step, cols), f32),
            pltpu.VMEM((cols // 128, 128, 128), f32),
            pltpu.SemaphoreType.DMA((rows // step,)),
            pltpu.SemaphoreType.DMA((cols // 128,)),
        ],
        cost_estimate=pl.CostEstimate(flops=0, bytes_accessed=rows * cols * 4, transcendentals=0),
        name="fill",
    )(prior2)


def batched(left, right):
    out = []
    for k in range(8):
        total = left[0][k : k + 1, :] * right[0]
        for e in range(1, 8):
            total = total + left[e][k : k + 1, :] * right[e]
        out.append(total)
    return out


def slabs(block):
    return [block[8 * e : 8 * e + 8, :] for e in range(8)]


def to_columns(rows):
    full = jnp.concatenate([rows, jnp.zeros((120, CH), f32)], axis=0)
    return full.T


def cholesky(a):
    row = iota((8, 128), 0)
    columns, scales = [], []
    a = list(a)
    for j in range(8):
        pivot = a[j][j : j + 1, :]
        scale = lax.rsqrt(pivot)
        scale = scale * (1.5 - 0.5 * pivot * scale * scale)
        column = jnp.where(row >= j, a[j] * scale, 0.0)
        for k in range(j + 1, 8):
            a[k] = a[k] - column * column[k : k + 1, :]
        columns.append(column)
        scales.append(scale)
    inverse = []
    for i in range(8):
        x = jnp.where(row == i, 1.0, 0.0)
        for j in range(i, 8):
            value = x[j : j + 1, :] * scales[j]
            x = jnp.where(row == j, value, jnp.where(row > j, x - columns[j] * value, x))
        inverse.append(x)
    return columns, inverse


def loop(count, body):
    if count == 1:
        body(0)
    else:
        lax.fori_loop(0, count, lambda at, carry: (body(at), carry)[1], 0)


def assemble_kernel(place, sizes, got_ref, prior_ref, filled_ref, out_ref,
                    jt, rows_s, cols_s, app, bt, placed, tiles, keys, squares,
                    listing, info, list_sm, info_sm, extra_sm, sem_list, sem_info, sem_out, sem_sq):
    del filled_ref
    rows, cols, chunks = sizes
    row_poses, col_poses, groups = rows // 8, cols // 8, cols // 128
    region, column = place()
    region_f, column_f = region.astype(f32), column.astype(f32)
    start = column * cols - region * rows
    own = (start >= 0) & (start < rows)
    per = CH // 8

    at_row, at_lane = iota((64, 1024), 0), iota((64, 1024), 1)
    expand = jnp.where(
        (at_row // 8 == at_lane // 128) & (at_row % 8 == at_lane % 8), 1.0, 0.0
    ).astype(bf16)

    sent = got_ref[0].astype(f32)[8:16, :]
    lane8, row8 = iota((8, 128), 1), iota((8, 128), 0)
    panel_prior = jnp.zeros((8, 128), f32)
    for at in range(3):
        panel_prior = panel_prior + pltpu.roll(sent, 128 - 32 * (at + 1), 1)
    panel_prior = jnp.where(lane8 < 32, panel_prior, 0.0)
    lined = jnp.zeros((8, 128), f32)
    for at in range(4):
        moved = panel_prior if at == 0 else pltpu.roll(panel_prior, 32 * at, 1)
        lined = lined + jnp.where(row8 % 4 == at, moved, 0.0)
    halves = [
        jnp.sum(jnp.where(row8 < 4, lined, 0.0), axis=0, keepdims=True),
        jnp.sum(jnp.where(row8 >= 4, lined, 0.0), axis=0, keepdims=True),
    ]
    prior_row = jnp.concatenate(halves, axis=1)
    kl, unknown = iota((64, PANEL), 0), iota((64, PANEL), 1)
    diagonal = jnp.where((kl // 8 == kl % 8) & (unknown % 8 == kl % 8), prior_row, 0.0)
    own_pose = jnp.where(iota((PANEL, 128), 0) // 8 == iota((PANEL, 128), 1), 1.0, 0.0).astype(bf16)
    first = dot(jnp.concatenate(split(diagonal, 3), axis=0), own_pose)
    first = first[0:64] + first[64:128] + first[128:192]
    kl = iota((64, 128), 0)
    spare = (kl // 8 == kl % 8) & (iota((64, 128), 1) >= PP)
    app[...] = first + jnp.where(spare, 1.0, 0.0)

    def measure(a):
        block = got_ref[pl.ds(a * per, per)].astype(f32)
        jac = block[:, 0:8, :].reshape(CH, 128)
        label = block[:, 8:16, :].reshape(CH, 128)
        jac_t = jac.T
        label_t = label.T
        jt[a] = jac_t
        d0, n0, d1, n1 = (label_t[at : at + 1, :] for at in range(4))
        c0 = d0 * row_poses + n0 - column_f * col_poses
        c1 = d1 * row_poses + n1 - column_f * col_poses
        one, none = jnp.ones_like(d0), jnp.zeros_like(d0)
        row0, row1 = d0 == region_f, d1 == region_f
        col0, col1 = (c0 >= 0) & (c0 < col_poses), (c1 >= 0) & (c1 < col_poses)
        pan0, pan1 = (d0 == 0) & (n0 < PP), (d1 == 0) & (n1 < PP)
        has_row = jnp.where(row0 | row1, one, none)
        has_col = jnp.where(col0 | col1, one, none)
        touches = jnp.where(pan0 | pan1, one, none)
        row_pose = jnp.where(row0, n0, n1)
        col_pose = jnp.where(col0, c0, c1)
        row_side = jnp.where(row0, none, one)
        col_side = jnp.where(col0, none, one)
        pan_side = jnp.where(pan0, none, one)
        pan_pose = jnp.where(pan0, n0, n1)
        row_in_panel = jnp.where((row0 & pan0) | (row1 & pan1), one, none)
        col_in_panel = jnp.where((col0 & pan0) | (col1 & pan1), one, none)
        relevant = has_row * has_col * (1.0 - row_in_panel)
        group = jnp.floor(col_pose * (1.0 / 16.0))
        within = col_pose - group * 16.0
        code = row_pose * groups + group
        is_row = touches * has_row * (1.0 - row_in_panel)
        is_col = touches * has_col * (1.0 - col_in_panel)
        lines = [
            jnp.where(relevant > 0, code, -1.0),
            jnp.where(relevant > 0, code, -2.0),
            jnp.where(touches > 0, pan_pose, -1.0),
            jnp.where(is_row > 0, pan_pose, -1.0),
            jnp.where(is_col > 0, pan_pose, -2.0),
            within,
            row_pose,
            group,
        ]
        more = [
            row_side, col_side, pan_side, relevant, col_in_panel,
            is_row * is_col, col_pose, none,
        ]
        lines, more = jnp.concatenate(lines, axis=0), jnp.concatenate(more, axis=0)
        rows_s[a] = jnp.concatenate([lines, more], axis=0)
        columns = to_columns(lines)
        cols_s[a] = columns
        j0, j1 = slabs(jac_t[0:64, :]), slabs(jac_t[64:128, :])
        near = [jnp.where(pan_side == 0, x, y) for x, y in zip(j0, j1)]
        gram = jnp.concatenate(batched(near, near), axis=0)
        of_pose = jnp.where(
            columns[:, 2:3] == iota((CH, 128), 1).astype(f32), 1.0, 0.0
        ).astype(bf16)
        total = dot(jnp.concatenate(split(gram, 3), axis=0), of_pose)
        app[...] += total[0:64] + total[64:128] + total[128:192]

    loop(chunks, measure)

    factor, inverse = cholesky(slabs(app[...]))
    factor = jnp.concatenate(factor, axis=0)
    inverse = jnp.concatenate(split(jnp.concatenate(inverse, axis=0), 3), axis=0)

    @pl.when((region == 0) & (column == 0))
    def _():
        swap = jnp.where(
            (at_row % 8 == at_lane // 128) & (at_row // 8 == at_lane % 8), 1.0, 0.0
        ).astype(bf16)
        full = jnp.concatenate([factor, jnp.zeros((64, 128), f32)], axis=0).T
        parts = [dot(part[0:PP, 0:64], swap) for part in split(full, 3)]
        value = parts[0] + parts[1] + parts[2]
        keep = iota((PP, 128), 1) // 8 == iota((PP, 128), 0) % 16
        for k in range(8):
            squares[pl.ds(k, PP, stride=8), :] = jnp.where(
                keep, value[:, 128 * k : 128 * k + 128], 0.0
            )
        for at in range(K_PANELS):
            piece = pl.ds(at * 128, 128)
            copy = pltpu.make_async_copy(
                squares.at[piece, :], out_ref.at[piece, piece], sem_sq.at[at]
            )
            copy.start()

    def blocks(a):
        row = [rows_s[a, at : at + 1, :] for at in range(16)]
        jac_t = jt[a]
        j0, j1 = slabs(jac_t[0:64, :]), slabs(jac_t[64:128, :])
        left = [jnp.where(row[8] == 0, x, y) for x, y in zip(j0, j1)]
        right = [jnp.where(row[9] == 0, x, y) for x, y in zip(j0, j1)]
        near = [jnp.where(row[10] == 0, x, y) for x, y in zip(j0, j1)]
        far = [jnp.where(row[10] == 0, y, x) for x, y in zip(j0, j1)]
        gram = batched(left, right)
        cross = batched(near, far)
        of_pose = jnp.where(iota((128, CH), 0).astype(f32) == row[2], 1.0, 0.0).astype(bf16)
        inv = dot(inverse, of_pose)
        inv = slabs(inv[0:64] + inv[64:128] + inv[128:192])
        solved = []
        for j in range(8):
            total = inv[0][j : j + 1, :] * cross[0]
            for i in range(1, j + 1):
                total = total + inv[i][j : j + 1, :] * cross[i]
            solved.append(total)
        bt[a] = jnp.concatenate(solved, axis=0)
        outer = batched(solved, solved)
        normal = [g - o * row[13] for g, o in zip(gram, outer)]
        keep_normal = row[11] * (1.0 - row[12])
        keep_panel = row[11] * row[12]
        normal = jnp.concatenate([x * keep_normal for x in normal], axis=0)
        panel = jnp.concatenate([x * keep_panel for x in solved], axis=0)
        both = jnp.concatenate([normal, panel], axis=0).T
        at_row2, at_lane2 = iota((128, 1024), 0), iota((128, 1024), 1)
        inner = at_row2 % 64
        straight = (inner // 8 == at_lane2 // 128) & (inner % 8 == at_lane2 % 8)
        turned = (inner % 8 == at_lane2 // 128) & (inner // 8 == at_lane2 % 8)
        table = jnp.where(
            ((at_row2 < 64) & straight) | ((at_row2 >= 64) & turned), 1.0, 0.0
        ).astype(bf16)
        columns = cols_s[a]
        keep = jnp.where((iota((CH, 128), 1) // 8).astype(f32) == columns[:, 5:6], 1.0, 0.0)
        keep = jnp.concatenate([keep] * 8, axis=1).astype(bf16)
        for at, part in enumerate(split(both, 2)):
            placed[a, at] = dot(part, table).astype(bf16) * keep

    loop(chunks, blocks)

    def merge(a):
        columns = cols_s[a]
        codes = jnp.broadcast_to(columns[:, 0:1], (CH, CH))
        line = rows_s[a]
        tiles_at = a * CH * 8
        before = iota((CH, CH), 0) < iota((CH, CH), 1)

        def from_chunk(b, repeats):
            same = jnp.where(codes == rows_s[b, 1:2, :], 1.0, 0.0).astype(bf16)
            total = dot(same, placed[b, 0]) + dot(same, placed[b, 1])
            other = jnp.broadcast_to(cols_s[b, :, 0:1], (CH, CH))
            earlier = jnp.where(other == line[1:2, :], 1.0, 0.0)
            if chunks == 1:
                earlier = jnp.where(before, earlier, 0.0)
            else:
                here = jnp.where(before, earlier, 0.0)
                factor_here = jnp.where(b == a, 1.0, 0.0)
                factor_all = jnp.where(b < a, 1.0, 0.0)
                earlier = here * factor_here + earlier * factor_all
            return total, repeats + jnp.sum(earlier, axis=0, keepdims=True)

        repeats = jnp.zeros((1, CH), f32)
        if chunks == 1:
            total, repeats = from_chunk(0, repeats)
        else:
            def step(b, carry):
                total, found = from_chunk(b, carry[1])
                return carry[0] + total, found
            total, repeats = lax.fori_loop(
                0, chunks, step, (jnp.zeros((CH, 1024), f32), repeats)
            )
        kept = jnp.where(repeats == 0, line[11:12, :], 0.0)
        upper = jnp.where(before, 1.0, 0.0).astype(bf16)
        rank = dot(jnp.broadcast_to(kept, (16, CH)).astype(bf16), upper)[0:1, :]
        chosen = jnp.where(
            (rank == iota((CH, CH), 0).astype(f32)) & (kept > 0), 1.0, 0.0
        ).astype(bf16)
        position = iota((1, CH), 1).astype(f32)
        data = jnp.concatenate(
            [line[6:7, :], line[7:8, :], position, jnp.zeros((13, CH), f32)], axis=0
        ).astype(bf16)
        found = dot(data, chosen, ((1,), (1,)))[0:8, :]
        count = jnp.sum(kept, axis=1, keepdims=True)
        row_at = iota((8, CH), 0)
        listing[a] = jnp.where(row_at == 3, count, found).astype(i32)
        pltpu.make_async_copy(listing.at[a], list_sm.at[a], sem_list.at[a]).start()
        info[a] = jnp.where(
            row_at == 0, line[6:7, :], jnp.where(row_at == 1, line[14:15, :], 0.0)
        ).astype(i32)
        pltpu.make_async_copy(info.at[a], info_sm.at[a], sem_info.at[a]).start()
        first_row = jnp.where(own, start // 128, 0)
        local = prior_ref[pl.ds(first_row, groups), :]
        share = jnp.where(own, 1.0, 0.0)
        group_of = columns[:, 7:8]
        base = jnp.zeros((CH, 128), f32)
        for at in range(groups):
            base = jnp.where(group_of == float(at), local[at : at + 1, :], base)
        base = base * share
        lane = iota((CH, 128), 1).astype(f32)
        offset = columns[:, 5:6] * 8.0
        for k in range(8):
            value = total[:, 128 * k : 128 * k + 128]
            value = value + jnp.where(lane == offset + float(k), base, 0.0)
            tiles[pl.ds(tiles_at + k, CH, stride=8), :] = value

    loop(chunks, merge)

    def waiting(a):
        pltpu.make_async_copy(listing.at[a], list_sm.at[a], sem_list.at[a]).wait()
        pltpu.make_async_copy(info.at[a], info_sm.at[a], sem_info.at[a]).wait()

    loop(chunks, waiting)

    lane_tile = iota((8, 128), 1)
    extra_sm[0] = 0

    def pairs(index):
        a, b = (0, 0) if chunks == 1 else (index // chunks, index % chunks)
        left = jnp.broadcast_to(cols_s[a, :, 3:4], (CH, CH))
        valid = left == rows_s[b, 4:5, :]
        same = iota((CH, CH), 0) == iota((CH, CH), 1)
        if chunks == 1:
            valid = valid & jnp.logical_not(same)
        else:
            valid = valid & jnp.logical_not(same & (a == b))
        key = (iota((CH, CH), 0) * CH + iota((CH, CH), 1)).astype(f32)
        key = jnp.where(valid, key, BIG)
        keys[...] = key
        smallest = jnp.min(key)

        def more(key_now):
            return key_now < BIG

        def one(key_now):
            number = key_now.astype(i32)
            m1, m2 = number // CH, number % CH
            r1, c2 = info_sm[a, 0, m1], info_sm[b, 1, m2]
            group, within = c2 // 16, c2 % 16
            position = iota((8, CH), 1)
            total = jnp.zeros((8, 128), f32)
            for j in range(8):
                x = bt[a, 8 * j : 8 * j + 8, :]
                y = bt[b, 8 * j : 8 * j + 8, :]
                x = jnp.sum(jnp.where(position == m1, x, 0.0), axis=1, keepdims=True)
                y = jnp.sum(jnp.where(position == m2, y, 0.0), axis=1, keepdims=True)
                y = jnp.where(lane_tile % 8 == row8, y, 0.0)
                y = jnp.sum(y, axis=0, keepdims=True)
                total = total + x * y
            total = jnp.where(lane_tile // 8 == within, -total, 0.0)

            def search(chunk, carry):
                def at_one(at, slot):
                    hit = (list_sm[chunk, 0, at] == r1) & (list_sm[chunk, 1, at] == group)
                    return jnp.where(hit, chunk * CH + list_sm[chunk, 2, at], slot)
                return lax.fori_loop(0, list_sm[chunk, 3, 0], at_one, carry)

            slot = search(0, -1) if chunks == 1 else lax.fori_loop(0, chunks, search, -1)
            added = extra_sm[0]
            code = r1 * groups + group

            def at_extra(at, slot):
                return jnp.where(extra_sm[1 + at] == code, chunks * CH + at, slot)

            slot = lax.fori_loop(0, added, at_extra, slot)

            @pl.when(slot >= 0)
            def _():
                where = pl.ds(pl.multiple_of(slot * 8, 8), 8)
                tiles[where, :] = tiles[where, :] + total

            @pl.when(slot < 0)
            def _():
                where = pl.ds(pl.multiple_of((chunks * CH + added) * 8, 8), 8)
                tiles[where, :] = total
                extra_sm[1 + added] = code
                extra_sm[0] = added + 1

            return jnp.min(jnp.where(keys[...] > key_now, keys[...], BIG))

        lax.while_loop(more, one, smallest)

    loop(chunks * chunks, pairs)

    def tile_copy(slot, r, group):
        return pltpu.make_async_copy(
            tiles.at[pl.ds(pl.multiple_of(slot * 8, 8), 8), :],
            out_ref.at[pl.ds(pl.multiple_of(r * 8, 8), 8), pl.ds(pl.multiple_of(group * 128, 128), 128)],
            sem_out,
        )

    def send(a):
        def one(at, carry):
            tile_copy(a * CH + list_sm[a, 2, at], list_sm[a, 0, at], list_sm[a, 1, at]).start()
            return carry
        lax.fori_loop(0, list_sm[a, 3, 0], one, 0)

    loop(chunks, send)

    def send_extra(at, carry):
        code = extra_sm[1 + at]
        tile_copy(chunks * CH + at, code // groups, code % groups).start()
        return carry

    lax.fori_loop(0, extra_sm[0], send_extra, 0)

    def drain_one(at, carry):
        tile_copy(0, 0, 0).wait()
        return carry

    def drain(a):
        lax.fori_loop(0, list_sm[a, 3, 0], drain_one, 0)

    loop(chunks, drain)
    lax.fori_loop(0, extra_sm[0], drain_one, 0)

    @pl.when((region == 0) & (column == 0))
    def _():
        for at in range(K_PANELS):
            piece = pl.ds(at * 128, 128)
            pltpu.make_async_copy(
                squares.at[piece, :], out_ref.at[piece, piece], sem_sq.at[at]
            ).wait()


def assemble(place, rows, cols, got, prior2, filled):
    count = got.shape[0] * 8
    chunks = count // CH
    capacity = rows // 8 * (cols // 128)
    any_space = pl.BlockSpec(memory_space=pl.ANY)
    vmem = pl.BlockSpec(memory_space=pltpu.VMEM)
    return pl.pallas_call(
        functools.partial(assemble_kernel, place, (rows, cols, chunks)),
        out_shape=jax.ShapeDtypeStruct((rows, cols), f32),
        in_specs=[vmem, vmem, any_space],
        out_specs=any_space,
        scratch_shapes=[
            pltpu.VMEM((chunks, 128, CH), f32),
            pltpu.VMEM((chunks, 16, CH), f32),
            pltpu.VMEM((chunks, CH, 128), f32),
            pltpu.VMEM((64, 128), f32),
            pltpu.VMEM((chunks, 64, CH), f32),
            pltpu.VMEM((chunks, 2, CH, 1024), bf16),
            pltpu.VMEM(((count + capacity) * 8, 128), f32),
            pltpu.VMEM((CH, CH), f32),
            pltpu.VMEM((PANEL, 128), f32),
            pltpu.VMEM((chunks, 8, CH), i32),
            pltpu.VMEM((chunks, 8, CH), i32),
            pltpu.SMEM((chunks, 8, CH), i32),
            pltpu.SMEM((chunks, 8, CH), i32),
            pltpu.SMEM((1 + capacity,), i32),
            pltpu.SemaphoreType.DMA((chunks,)),
            pltpu.SemaphoreType.DMA((chunks,)),
            pltpu.SemaphoreType.DMA,
            pltpu.SemaphoreType.DMA((K_PANELS,)),
        ],
        input_output_aliases={2: 0},
        compiler_params=pltpu.CompilerParams(vmem_limit_bytes=48 << 20),
        name="assemble",
    )(got, prior2, filled)


def place():
    return lax.axis_index("region"), lax.axis_index("col")


def body(jac, dest, near_pose, prior):
    regions, columns = lax.axis_size("region"), lax.axis_size("col")
    devices = regions * columns
    rows = prior.shape[0]
    cols = rows * regions // columns
    assert jac.shape[0] == 8 and devices * 8 % CH == 0
    assert rows % cols == 0 and rows // 8 <= 256 and regions <= 256
    assert rows >= PANEL and cols >= PANEL and cols % 128 == 0
    prior2 = prior.reshape(rows // 128, 128)
    packed = pack(jac, dest, near_pose, prior2, devices)
    got = lax.all_to_all(packed, ("region", "col"), split_axis=0, concat_axis=0, tiled=True)
    filled = fill(place, rows, cols, prior2)
    return assemble(place, rows, cols, got, prior2, filled)


def solution(mesh):
    return jax.shard_map(
        body,
        mesh=mesh,
        in_specs=(
            P(("region", "col"), None),
            P(("region", "col"), None),
            P(("region", "col"), None),
            P("region"),
        ),
        out_specs=P("region", "col"),
        check_vma=False,
    )
```

time: 654 us -> 24.4 us (0.04)
  local copies, waits for them, and re-layouts: 238 us -> 2.7 us
  waiting for transfers between devices: 189 us -> 3.17 us
  other arithmetic: 129 us -> 0 us
  matrix products: 44 us -> 0 us
  blocking collectives: 28.2 us -> 0 us
  between operations: 13.6 us -> 0.02 us
  Pallas kernels: 0 us -> 10.9 us
    convert_element_type x5 -> x0, local copies, waits for them, and re-layouts: 214 us -> none  [the longest x2 213 us: placed(): summed.astype(jnp.bfloat16).reshape(blocks.shape[0] * 8, pose_count * 8)]
    psum x2 -> x0, waiting for transfers between devices: 115 us -> none  [broadcast(): return lax.psum(block, axis)]
    convert_element_type x8 -> x0, other arithmetic: 71.7 us -> none  [the longest x2 66.7 us: placed(): summed.astype(jnp.bfloat16).reshape(blocks.shape[0] * 8, pose_count * 8)]
    all_gather x2 -> x0, waiting for transfers between devices: 70.4 us -> none  [body(): lax.all_gather(panel_part.astype(jnp.bfloat16), 'region', axis=0, tiled=T...]
    another operation x15 -> x0, other arithmetic: 48.5 us -> none  [the longest x6 24.9 us: body(): factor = jnp.tril(jnp.linalg.cholesky(diagonal))]
    dot_general x5 -> x0, matrix products: 38.5 us -> none  [the longest x2 28.7 us: body(): matrix = matrix - jnp.dot(mine, theirs.T, precision=lax.Precision.HIGHEST)]
    all_gather x2 -> x0, blocking collectives: 28.2 us -> none  [the longest x1 14.2 us: body(): piece_labels = lax.all_gather(arrived_labels, 'col', axis=0, tiled=True)]
    pallas_call x0 -> x3, Pallas kernels: none -> 10.9 us  [the longest x1 4.98 us: fill(): pl.pallas_call(functools.partial(fill_kernel, place, (rows, cols)), out_s...]
  transfers between devices with their start and end apart: 6 -> 1, of which waited for: 5 -> 1; matrix products, arithmetic and copies ran while one was open for 1% -> 0% of each run, Pallas kernels for 0% -> 21%
where the time goes in v1:
time: 24.4 us; the launch traced here: 24.1 us
  Pallas kernels  10.9 us (45%)
  starting transfers between devices  7.33 us (30%)
  waiting for transfers between devices  3.17 us (13%)
  local copies, waits for them, and re-layouts  2.7 us (11%)
    all_to_all x1, starting transfers between devices, body(): lax.all_to_all(packed, ('region', 'col'), split_axis=0, concat_axis=0, ti...  7.33 us
    pallas_call x1, Pallas kernels, fill(): pl.pallas_call(functools.partial(fill_kernel, place, (rows, cols)), out_s...  4.98 us
    pallas_call x1, Pallas kernels, assemble(): pl.pallas_call(functools.partial(assemble_kernel, place, (rows, cols, chu...  4.38 us
    all_to_all x1, waiting for transfers between devices, body(): lax.all_to_all(packed, ('region', 'col'), split_axis=0, concat_axis=0, ti...  3.17 us
    unnamed x4, local copies, waits for them, and re-layouts  2.7 us
    pallas_call x1, Pallas kernels, pack(): pl.pallas_call(pack_kernel, out_shape=jax.ShapeDtypeStruct((devices, 16,...  1.54 us
  transfers between devices with their start and end apart: 1, of which 1 were waited for; matrix products, arithmetic and copies ran while one was open for 0% of the time, Pallas kernels for 21%

profile of v1, /device:TPU:0, one launch (start us, length us, event | category | flops | bytes accessed | tf_op | source)
XLA Modules:
  0.0 24.1 jit_solution(9829430189016354385)
XLA Ops:
  0.0 0.0 copy-start
  0.0 1.4 %copy.6.dest_ref = s32[8,2]{1,0:T(8,128)} copy(s32[8,2]{0,1:T(2,128)} %param.5) | data formatting | bytes 128 | tf_op args[1]
  1.4 1.3 %copy.7.near_ref = s32[8,2]{1,0:T(8,128)} copy(s32[8,2]{0,1:T(2,128)} %param.6) | data formatting | bytes 128 | tf_op args[2]
  2.7 1.5 %pack.1 = bf16[32,16,128]{2,1,0:T(8,128)(2,1)} custom-call(bf16[8,128]{1,0:T(8,128)(2,1)} %jac_ref.1, s32[8,2]{1,0:T(8,128)} %copy.6.dest_ref, s32[8,2]{1,0:T(8,128)} %copy.7.near_ref, f32[16,128]{1,0:T(8,128)} %bitcast.1), custom_call_target="tpu_custom_call" | custom-call | tf_op jit(solution)/shard_map/pack/pallas_call | solution.py:57
  4.2 7.3 %all-to-all-start = ((bf16[32,16,128]{2,1,0:T(8,128)(2,1)}), bf16[32,16,128]{2,1,0:T(8,128)(2,1)S(1)}, u32[]{:S(2)}, u32[]{:S(2)}) async-start(bf16[32,16,128]{2,1,0:T(8,128)(2,1)} %pack.1), calls=%async_computation | async-start | bytes 262144 | tf_op jit(solution)/shard_map/all_to_all | solution.py:574
  11.6 5.0 %fill.1.filled_ref = f32[2048,1024]{1,0:T(8,128)} custom-call(f32[16,128]{1,0:T(8,128)} %bitcast.2), custom_call_target="tpu_custom_call" | custom-call | bytes 8388608 | tf_op jit(solution)/shard_map/fill/pallas_call | solution.py:108
  16.6 3.2 %all-to-all-done.got_ref = bf16[32,16,128]{2,1,0:T(8,128)(2,1)S(1)} async-done(((bf16[32,16,128]{2,1,0:T(8,128)(2,1)}), bf16[32,16,128]{2,1,0:T(8,128)(2,1)S(1)}, u32[]{:S(2)}, u32[]{:S(2)}) %all-to-all-start) | async-done | bytes 131104 | tf_op jit(solution)/shard_map/all_to_all | solution.py:574
  19.7 0.0 copy-done
  19.7 4.4 %assemble.1 = f32[2048,1024]{1,0:T(8,128)} custom-call(bf16[32,16,128]{2,1,0:T(8,128)(2,1)S(1)} %all-to-all-done.got_ref, f32[16,128]{1,0:T(8,128)S(1)} %bitcast.3, f32[2048,1024]{1,0:T(8,128)} %fill.1.filled_ref), custom_call_target="tpu_custom_call", output_to_operand_aliasing={{}: (2, {})} | custom-call | tf_op jit(solution)/shard_map/assemble/pallas_call | solution.py:529
Async XLA Ops:
  0.0 19.7 %copy-start = (f32[2048]{0:T(1024)S(1)}, f32[2048]{0:T(1024)}, u32[]{:S(2)}) copy-start(f32[2048]{0:T(1024)} %param.7) | copy-start | bytes 24580
  4.2 15.5 %all-to-all-start = ((bf16[32,16,128]{2,1,0:T(8,128)(2,1)}), bf16[32,16,128]{2,1,0:T(8,128)(2,1)S(1)}, u32[]{:S(2)}, u32[]{:S(2)}) async-start(bf16[32,16,128]{2,1,0:T(8,128)(2,1)} %pack.1), calls=%async_computation | async-start | bytes 262144 | tf_op jit(solution)/shard_map/all_to_all | solution.py:574

commit v2 on v1

--- a/solution.py
+++ b/solution.py
@@ -38,7 +38,9 @@
     lane, row = iota(shape, 1), iota(shape, 0)
     dest, near = dest_ref[...].astype(f32), near_ref[...].astype(f32)
     tile = jnp.zeros(shape, f32)
-    for at, column in enumerate((dest[:, 0:1], near[:, 0:1], dest[:, 1:2], near[:, 1:2])):
+    corner = iota((8, 8), 0) == iota((8, 8), 1)
+    for at, line in enumerate((dest[0:1, :], near[0:1, :], dest[1:2, :], near[1:2, :])):
+        column = jnp.sum(jnp.where(corner, line, 0.0), axis=1, keepdims=True)
         tile = jnp.where(lane == at, column, tile)
     first = prior_ref[0:2, :]
     both = jnp.where(row < 4, first[0:1, :], first[1:2, :])
@@ -57,8 +59,10 @@
     return pl.pallas_call(
         pack_kernel,
         out_shape=jax.ShapeDtypeStruct((devices, 16, 128), bf16),
+        in_specs=[pl.BlockSpec(memory_space=pltpu.VMEM)] * 4,
+        out_specs=pl.BlockSpec(memory_space=pltpu.VMEM),
         name="pack",
-    )(jac, dest, near_pose, prior2)
+    )(jac, dest.T, near_pose.T, prior2)
 
 
 def fill_kernel(place, sizes, prior_ref, out_ref, zeros, squares, sem, sem2):

time: 24.4 us -> 21.7 us (0.89)
  local copies, waits for them, and re-layouts: 2.7 us -> 0.01 us
    unnamed x4 -> x2, local copies, waits for them, and re-layouts: 2.7 us -> 0.01 us
  transfers between devices with their start and end apart: 1 -> 1, of which waited for: 1 -> 1; matrix products, arithmetic and copies ran while one was open for 0% -> 0% of each run, Pallas kernels for 21% -> 23%
where the time goes in v2:
time: 21.7 us; the launch traced here: 21.5 us
  Pallas kernels  10.9 us (50%)
  starting transfers between devices  7.33 us (34%)
  waiting for transfers between devices  3.17 us (15%)
    all_to_all x1, starting transfers between devices, body(): lax.all_to_all(packed, ('region', 'col'), split_axis=0, concat_axis=0, ti...  7.33 us
    pallas_call x1, Pallas kernels, fill(): pl.pallas_call(functools.partial(fill_kernel, place, (rows, cols)), out_s...  4.98 us
    pallas_call x1, Pallas kernels, assemble(): pl.pallas_call(functools.partial(assemble_kernel, place, (rows, cols, chu...  4.38 us
    all_to_all x1, waiting for transfers between devices, body(): lax.all_to_all(packed, ('region', 'col'), split_axis=0, concat_axis=0, ti...  3.17 us
    pallas_call x1, Pallas kernels, pack(): pl.pallas_call(pack_kernel, out_shape=jax.ShapeDtypeStruct((devices, 16,...  1.57 us
  transfers between devices with their start and end apart: 1, of which 1 were waited for; matrix products, arithmetic and copies ran while one was open for 0% of the time, Pallas kernels for 23%

profile of v2, /device:TPU:0, one launch (start us, length us, event | category | flops | bytes accessed | tf_op | source)
XLA Modules:
  0.0 21.5 jit_solution(17599242754844614888)
XLA Ops:
  0.0 0.0 copy-start
  0.0 1.6 %pack.1 = bf16[32,16,128]{2,1,0:T(8,128)(2,1)} custom-call(bf16[8,128]{1,0:T(8,128)(2,1)} %jac_ref.1, s32[2,8]{1,0:T(2,128)} %bitcast.6, s32[2,8]{1,0:T(2,128)} %bitcast.7, f32[16,128]{1,0:T(8,128)} %bitcast.3), custom_call_target="tpu_custom_call" | custom-call | tf_op jit(solution)/shard_map/pack/pallas_call | solution.py:59
  1.6 7.3 %all-to-all-start = ((bf16[32,16,128]{2,1,0:T(8,128)(2,1)}), bf16[32,16,128]{2,1,0:T(8,128)(2,1)S(1)}, u32[]{:S(2)}, u32[]{:S(2)}) async-start(bf16[32,16,128]{2,1,0:T(8,128)(2,1)} %pack.1), calls=%async_computation | async-start | bytes 262144 | tf_op jit(solution)/shard_map/all_to_all | solution.py:578
  8.9 5.0 %fill.1.filled_ref = f32[2048,1024]{1,0:T(8,128)} custom-call(f32[16,128]{1,0:T(8,128)} %bitcast.4), custom_call_target="tpu_custom_call" | custom-call | bytes 8388608 | tf_op jit(solution)/shard_map/fill/pallas_call | solution.py:112
  13.9 3.2 %all-to-all-done.got_ref = bf16[32,16,128]{2,1,0:T(8,128)(2,1)S(1)} async-done(((bf16[32,16,128]{2,1,0:T(8,128)(2,1)}), bf16[32,16,128]{2,1,0:T(8,128)(2,1)S(1)}, u32[]{:S(2)}, u32[]{:S(2)}) %all-to-all-start) | async-done | bytes 131104 | tf_op jit(solution)/shard_map/all_to_all | solution.py:578
  17.1 0.0 copy-done
  17.1 4.4 %assemble.1 = f32[2048,1024]{1,0:T(8,128)} custom-call(bf16[32,16,128]{2,1,0:T(8,128)(2,1)S(1)} %all-to-all-done.got_ref, f32[16,128]{1,0:T(8,128)S(1)} %bitcast.5, f32[2048,1024]{1,0:T(8,128)} %fill.1.filled_ref), custom_call_target="tpu_custom_call", output_to_operand_aliasing={{}: (2, {})} | custom-call | tf_op jit(solution)/shard_map/assemble/pallas_call | solution.py:533
Async XLA Ops:
  0.0 17.1 %copy-start = (f32[2048]{0:T(1024)S(1)}, f32[2048]{0:T(1024)}, u32[]{:S(2)}) copy-start(f32[2048]{0:T(1024)} %param.7) | copy-start | bytes 24580
  1.6 15.5 %all-to-all-start = ((bf16[32,16,128]{2,1,0:T(8,128)(2,1)}), bf16[32,16,128]{2,1,0:T(8,128)(2,1)S(1)}, u32[]{:S(2)}, u32[]{:S(2)}) async-start(bf16[32,16,128]{2,1,0:T(8,128)(2,1)} %pack.1), calls=%async_computation | async-start | bytes 262144 | tf_op jit(solution)/shard_map/all_to_all | solution.py:578
